TPU v7x, 32 devices: a whole 2x2x4 slice. The times are simulated.
32 devices in a mesh: groups: 2 (over x), rows: 16 (over z, y, core).
Axes of the slice: x: 2, y: 2, z: 4, core: 2. Of those that a mesh axis runs over, the one named last changes fastest.
Arguments:
- points: bfloat16 [64, 32768], P(None, ('groups', 'rows')), parts along dimension 1, may hold values from -12 to 12
- landmarks: bfloat16 [64, 2048], P(None, 'groups'), parts along dimension 1, may hold values from -12 to 12
- chol: float32 [2048, 1024], P('groups'), parts along dimension 0
- ridge: float32 [2], P('groups'), parts along dimension 0, may hold values from 0.5 to 2
- solution: float32 [8, 32768], P(None, ('groups', 'rows')), parts along dimension 1, may hold values from -6 to 6
- residual: float32 [8, 32768], P(None, ('groups', 'rows')), parts along dimension 1, may hold values from -6 to 6
- direction: float32 [8, 32768], P(None, ('groups', 'rows')), parts along dimension 1, may hold values from -6 to 6
- rz_prev: float32 [16], P('groups'), parts along dimension 0, may hold values from 8192 to 32768
Outputs:
- solution_new: float32 [8, 32768], P(None, ('groups', 'rows')), parts along dimension 1
- residual_new: float32 [8, 32768], P(None, ('groups', 'rows')), parts along dimension 1
- direction_new: float32 [8, 32768], P(None, ('groups', 'rows')), parts along dimension 1
- inner_new: float32 [16], P('groups'), parts along dimension 0
There are 2 independent parts, one for each index of `groups`. A program takes and returns all parts, laid end to end along the dimension named above; each array names one. Nothing has to cross between parts.
All inputs are finite; a program needn't handle non-finite values.
Results may differ from a plain program's by a relative error of at most 0.0064.
Values may be sent and summed in bfloat16 or wider, within the bound.
A program may use at most 64 MiB of HBM per device.

v0:
```python
import math

import jax
import jax.numpy as jnp
from jax import lax
from jax.sharding import PartitionSpec as P


def square_norms(features):
    wide = features.astype(jnp.float32)
    return jnp.sum(wide * wide, axis=0)


def kernel_block(row_points, row_norms, col_points, col_norms):
    scale = 0.5 / row_points.shape[0]
    cross = lax.dot_general(
        row_points, col_points, (((0,), (0,)), ((), ())), preferred_element_type=jnp.float32
    )
    dist = row_norms[:, None] + col_norms[None, :] - 2.0 * cross
    return jnp.exp(-scale * dist)


def split_blocks(values, block_len):
    blocks = values.shape[-1] // block_len
    return jnp.moveaxis(values.reshape(values.shape[:-1] + (blocks, block_len)), -2, 0)


def row_products(own_points, own_norms, col_points, col_dirs):
    block_len = math.gcd(col_points.shape[1], 4096)
    point_blocks = split_blocks(col_points, block_len)
    dir_blocks = split_blocks(col_dirs, block_len)

    def step_block(running, inputs):
        block_points, block_dirs = inputs
        kernel_tile = kernel_block(
            own_points, own_norms, block_points, square_norms(block_points)
        ).astype(jnp.bfloat16)
        added = lax.dot_general(
            block_dirs, kernel_tile, (((1,), (1,)), ((), ())), preferred_element_type=jnp.float32
        )
        return (running + added, None)

    start_value = jnp.zeros((col_dirs.shape[0], own_points.shape[1]), jnp.float32)
    summed, _ = lax.scan(step_block, start_value, (point_blocks, dir_blocks))
    return summed


def precondition(residual, landmark_kernel, projection, chol, ridge_value):
    coeffs = jax.scipy.linalg.cho_solve((chol, True), projection.T)
    precond = (
        residual - jnp.dot(coeffs.T, landmark_kernel.T, precision=lax.Precision.HIGHEST)
    ) / ridge_value
    return (coeffs, precond)


def local(points, landmarks, chol, ridge, solution, residual, direction, rz_prev):
    ridge_value = ridge[0]
    norms = square_norms(points)
    landmark_kernel = kernel_block(points, norms, landmarks, square_norms(landmarks))
    partial_proj = jnp.dot(residual, landmark_kernel, precision=lax.Precision.HIGHEST)
    projection = lax.psum(partial_proj, "rows")
    coeffs, precond = precondition(residual, landmark_kernel, projection, chol, ridge_value)
    inner_new = lax.psum(jnp.sum(precond * residual, axis=1), "rows")
    direction_new = precond + (inner_new / rz_prev)[:, None] * direction
    direction_low = direction_new.astype(jnp.bfloat16)
    kernel_part = row_products(
        points,
        norms,
        lax.all_gather(points, "rows", axis=1, tiled=True),
        lax.all_gather(direction_low, "rows", axis=1, tiled=True),
    )
    image = kernel_part + ridge_value * direction_new
    curvature = lax.psum(jnp.sum(direction_new * image, axis=1), "rows")
    alpha = inner_new / curvature
    solution_new = solution + alpha[:, None] * direction_new
    residual_new = residual - alpha[:, None] * image
    return (solution_new, residual_new, direction_new, inner_new)


def solution(mesh):
    in_specs = (
        P(None, ("groups", "rows")),
        P(None, "groups"),
        P("groups", None),
        P("groups"),
        P(None, ("groups", "rows")),
        P(None, ("groups", "rows")),
        P(None, ("groups", "rows")),
        P("groups"),
    )
    out_specs = (
        P(None, ("groups", "rows")),
        P(None, ("groups", "rows")),
        P(None, ("groups", "rows")),
        P("groups"),
    )
    return jax.shard_map(local, mesh=mesh, in_specs=in_specs, out_specs=out_specs, check_vma=False)
```

profile of v0, /device:TPU:0, one launch (start us, length us, event | category | flops | bytes accessed | tf_op | source)
XLA Modules:
  0.0 328.2 jit_solution(10841898238312821311)
XLA Ops:
  7.2 0.7 all-gather.2.cloned.1.call-update
  7.9 1.1 multiply_reduce_fusion.2
  9.0 3.8 %fusion.100 = f32[1024,1024]{1,0:T(8,128)} fusion(bf16[64,1024]{1,0:T(8,128)(2,1)} %param.10, bf16[64,1024]{1,0:T(8,128)(2,1)} %param.11), kind=kOutput, calls=%fused_computation.178 | convolution fusion | flops 134217728 | bytes 4456448 | tf_op jit(solution)/shard_map/dot_general | solution.py:16
  12.9 2.4 fusion.15
  15.4 23.2 %while.12 = (s32[]{:T(128)}, f32[1024,1024]{1,0:T(8,128)}, s32[8,2]{0,1:T(2,128)S(1)}, f32[8,128,128]{2,1,0:T(8,128)S(1)}, s32[]{:T(128)}) while((s32[]{:T(128)}, f32[1024,1024]{1,0:T(8,128)}, s32[8,2]{0,1:T(2,128)S(1)}, f32[8,128,128]{2,1,0:T(8,128)S(1)}, s32[]{:T(128)}) %tuple.65), condition=%wide.while_cond, body=%wide.while_body.sunk | while | flops 2 | bytes 131181 | solution.py:49
  15.4 0.5 fusion.134
  16.0 2.3 bitcast_dynamic-update-slice_fusion.2
  18.4 0.5 fusion.134
  18.9 2.3 bitcast_dynamic-update-slice_fusion.2
  21.3 0.5 fusion.134
  21.8 2.3 bitcast_dynamic-update-slice_fusion.2
  24.2 0.5 fusion.134
  24.7 2.3 bitcast_dynamic-update-slice_fusion.2
  27.1 0.5 fusion.134
  27.6 2.3 bitcast_dynamic-update-slice_fusion.2
  30.0 0.5 fusion.134
  30.5 2.3 bitcast_dynamic-update-slice_fusion.2
  32.9 0.5 fusion.134
  33.4 2.3 bitcast_dynamic-update-slice_fusion.2
  35.8 0.5 fusion.134
  36.3 2.2 bitcast_dynamic-update-slice_fusion.2
  38.6 78.6 %custom-call.7 = f32[8,128,128]{1,2,0:T(8,128)S(1)} custom-call(f32[8,128,128]{2,1,0:T(8,128)S(1)} %get-tuple-element.44), custom_call_target="InvertDiagBlocksLowerTriangular" | custom-call | tf_op jit(solution)/shard_map/jit(_cho_solve)/triangular_solve | solution.py:49
  117.2 5.3 %fusion.17 = f32[1024,8]{0,1:T(8,128)S(1)} fusion(f32[8,1024]{1,0:T(8,128)S(1)} %copy-done.6, f32[1024,1024]{1,0:T(8,128)} %fusion.100, f32[1024]{0:T(1024)S(1)} %multiply_reduce_fusion.1, f32[1024]{0:T(1024)S(1)} %multiply_reduce_fusion.2), kind=kOutput, calls=%fused_computation.20 | convolution fusion | flops 104857600 | bytes 4268032 | tf_op jit(solution)/shard_map/dot_general | solution.py:60
  122.5 63.0 %psum.21 = f32[1024,8]{0,1:T(8,128)S(1)} all-reduce(f32[1024,8]{0,1:T(8,128)S(1)} %fusion.17), channel_id=1, replica_groups=mesh['groups'=2,'rows'=16] {'rows'}, use_global_device_ids=true, to_apply=%region_2.0 | all-reduce | flops 8192 | bytes 65536 | tf_op jit(solution)/shard_map/psum | solution.py:61
  185.7 1.2 convolution_subtract_fusion.9
  186.9 0.2 constant_dynamic-update-slice_fusion.9
  187.1 1.1 convolution_subtract_fusion.8
  188.2 0.2 constant_dynamic-update-slice_fusion.8
  188.4 1.2 convolution_subtract_fusion.7
  189.6 0.2 constant_dynamic-update-slice_fusion.7
  189.8 1.2 convolution_subtract_fusion.6
  191.0 0.2 constant_dynamic-update-slice_fusion.6
  191.2 1.4 convolution_subtract_fusion.5
  192.6 0.2 constant_dynamic-update-slice_fusion.5
  192.8 1.4 convolution_subtract_fusion.13
  194.2 0.2 constant_dynamic-update-slice_fusion.11
  194.4 1.5 convolution_subtract_fusion.12
  195.9 0.3 fusion.56
  196.2 0.2 fusion.55
  196.5 1.0 convolution_subtract_fusion.4
  197.5 0.2 fusion.53
  197.7 1.1 convolution_subtract_fusion.3
  198.8 0.2 fusion.51
  199.0 1.2 convolution_subtract_fusion.2
  200.2 0.2 fusion.49
  200.4 1.2 convolution_subtract_fusion.1
  201.6 0.2 constant_dynamic-update-slice_fusion.22
  201.9 1.3 convolution_subtract_fusion
  204.1 1.3 convolution_subtract_fusion.11
  205.4 0.2 constant_dynamic-update-slice_fusion.35
  205.7 1.4 convolution_subtract_fusion.10
  207.1 0.2 convolution_dynamic-update-slice_fusion
  207.4 4.2 %multiply_reduce_fusion.4 = (f32[8]{0:T(128)S(1)}, f32[8,1024]{1,0:T(8,128)S(1)}) fusion(f32[8,1024]{1,0:T(8,128)S(1)} %copy-done.6, f32[]{:T(128)} %bitcast.125, f32[1024,8]{0,1:T(8,128)S(1)} %constant_dynamic-update-slice_fusion.36, f32[1024,1024]{1,0:T(8,128)S(1)} %copy-done.1, f32[1024]{0:T(1024)S(1)} %multiply_reduce_fusion.1, ...), kind=kOutput, calls=%fused_computation.133 | convolution fusion | flops 104890360 | bytes 4300836 | tf_op jit(solution)/shard_map/dot_general | solution.py:51
  211.6 29.5 %psum.22 = f32[8]{0:T(128)S(1)} all-reduce(f32[8]{0:T(128)S(1)} %get-tuple-element.129), channel_id=1, replica_groups=mesh['groups'=2,'rows'=16] {'rows'}, use_global_device_ids=true, to_apply=%region_4.5 | all-reduce | flops 8 | bytes 64 | tf_op jit(solution)/shard_map/psum | solution.py:63
  241.2 18.1 %all_gather.6 = bf16[8,16384]{1,0:T(8,128)(2,1)S(1)} all-gather(bf16[8,1024]{1,0:T(8,128)(2,1)S(1)} %get-tuple-element.92), channel_id=1, replica_groups=mesh['groups'=2,'rows'=16] {'rows'}, dimensions={1}, use_global_device_ids=true | all-gather | bytes 278528 | tf_op jit(solution)/shard_map/all_gather | solution.py:70
  259.3 4.5 %reshape.69 = bf16[64,4,4096]{2,1,0:T(4,128)(2,1)} reshape(bf16[64,16384]{1,0:T(8,128)(2,1)} %all-gather.2.cloned.1.call-done) | data formatting | bytes 4194304 | tf_op jit(solution)/shard_map/reshape | solution.py:25
  263.8 2.7 copy.12
  266.6 22.5 %while.13 = (s32[]{:T(128)}, f32[8,1024]{1,0:T(8,128)S(1)}, bf16[4,8,4096]{2,1,0:T(8,128)(2,1)S(1)}, f32[1024]{0:T(1024)S(1)}, bf16[4,64,4096]{2,1,0:T(8,128)(2,...) while((s32[]{:T(128)}, f32[8,1024]{1,0:T(8,128)S(1)}, ...), condition=%wide.region_7.8_spmd.clone, body=%wide.region_5.7_spmd.clone.sunk | while | flops 625750016 | bytes 1348707 | solution.py:44
  266.7 5.5 %fusion.138 = f32[8,1024]{1,0:T(8,128)S(1)} fusion(bf16[64,1024]{1,0:T(8,128)(2,1)S(1)} %get-tuple-element.233, f32[4096]{0:T(1024)S(1)} %multiply_reduce_fusion.6, f32[1024]{0:T(1024)S(1)} %get-tuple-element.231, bf16[4,64,4096]{2,1,0:T(8,128)(2,1)S(1)} %get-tuple-element.232, s32[]{:T(128)} %get-tuple-element.220, ...), kind=kOutput, calls=%fused_computation.7.clone.1 | convolution fusion | flops 624967680 | bytes 807937 | tf_op jit(solution)/shard_map/while/body/eval_jaxpr/dot_general | solution.py:38
  272.4 5.5 %fusion.138 = f32[8,1024]{1,0:T(8,128)S(1)} fusion(bf16[64,1024]{1,0:T(8,128)(2,1)S(1)} %get-tuple-element.233, f32[4096]{0:T(1024)S(1)} %multiply_reduce_fusion.6, f32[1024]{0:T(1024)S(1)} %get-tuple-element.231, bf16[4,64,4096]{2,1,0:T(8,128)(2,1)S(1)} %get-tuple-element.232, s32[]{:T(128)} %get-tuple-element.220, ...), kind=kOutput, calls=%fused_computation.7.clone.1 | convolution fusion | flops 624967680 | bytes 807937 | tf_op jit(solution)/shard_map/while/body/eval_jaxpr/dot_general | solution.py:38
  278.0 5.5 %fusion.138 = f32[8,1024]{1,0:T(8,128)S(1)} fusion(bf16[64,1024]{1,0:T(8,128)(2,1)S(1)} %get-tuple-element.233, f32[4096]{0:T(1024)S(1)} %multiply_reduce_fusion.6, f32[1024]{0:T(1024)S(1)} %get-tuple-element.231, bf16[4,64,4096]{2,1,0:T(8,128)(2,1)S(1)} %get-tuple-element.232, s32[]{:T(128)} %get-tuple-element.220, ...), kind=kOutput, calls=%fused_computation.7.clone.1 | convolution fusion | flops 624967680 | bytes 807937 | tf_op jit(solution)/shard_map/while/body/eval_jaxpr/dot_general | solution.py:38
  283.6 5.5 %fusion.138 = f32[8,1024]{1,0:T(8,128)S(1)} fusion(bf16[64,1024]{1,0:T(8,128)(2,1)S(1)} %get-tuple-element.233, f32[4096]{0:T(1024)S(1)} %multiply_reduce_fusion.6, f32[1024]{0:T(1024)S(1)} %get-tuple-element.231, bf16[4,64,4096]{2,1,0:T(8,128)(2,1)S(1)} %get-tuple-element.232, s32[]{:T(128)} %get-tuple-element.220, ...), kind=kOutput, calls=%fused_computation.7.clone.1 | convolution fusion | flops 624967680 | bytes 807937 | tf_op jit(solution)/shard_map/while/body/eval_jaxpr/dot_general | solution.py:38
  289.2 31.5 %psum.23 = f32[8]{0:T(128)S(1)} all-reduce(f32[8]{0:T(128)S(1)} %multiply_reduce_fusion.3), channel_id=1, replica_groups=mesh['groups'=2,'rows'=16] {'rows'}, use_global_device_ids=true, to_apply=%region_9.10 | all-reduce | flops 8 | bytes 64 | tf_op jit(solution)/shard_map/psum | solution.py:73
  320.7 0.7 multiply_subtract_fusion
  (67 shorter events, 2.1 us)
Async XLA Ops:
  7.2 5.7 %copy-start.3 = (bf16[64,1024]{1,0:T(8,128)(2,1)S(1)}, bf16[64,1024]{1,0:T(8,128)(2,1)}, u32[]{:S(2)}) copy-start(bf16[64,1024]{1,0:T(8,128)(2,1)} %param.11) | copy-start | bytes 393220
  7.2 252.1 %all-gather.2.cloned.1.call-start = ((), (), s32[]{:S(2)}) async-start(), calls=%async_computation | async-start | bytes 2228224 | tf_op jit(solution)/shard_map/all_gather | solution.py:69
  7.9 5.0 %copy-start = (f32[1024,1024]{1,0:T(8,128)S(1)}, f32[1024,1024]{1,0:T(8,128)}, u32[]{:S(2)}) copy-start(f32[1024,1024]{1,0:T(8,128)} %param.12) | copy-start | bytes 12582916
  12.9 104.3 %copy-start.6 = (f32[8,1024]{1,0:T(8,128)S(1)}, f32[8,1024]{1,0:T(8,128)}, u32[]{:S(2)}) copy-start(f32[8,1024]{1,0:T(8,128)} %param.15) | copy-start | bytes 98308
  185.5 21.8 %copy-start.1 = (f32[1024,1024]{1,0:T(8,128)S(1)}, f32[1024,1024]{1,0:T(8,128)}, u32[]{:S(2)}) copy-start(f32[1024,1024]{1,0:T(8,128)} %fusion.100) | copy-start | bytes 12582916
  195.9 45.1 %copy-start.8 = (f32[8]{0:T(128)S(1)}, f32[8]{0:T(128)}, u32[]{:S(2)}) copy-start(f32[8]{0:T(128)} %param.17) | copy-start | bytes 100
  195.9 45.1 %copy-start.5 = (f32[8,1024]{1,0:T(8,128)S(1)}, f32[8,1024]{1,0:T(8,128)}, u32[]{:S(2)}) copy-start(f32[8,1024]{1,0:T(8,128)} %param.16) | copy-start | bytes 98308
  241.1 79.6 %copy-start.9 = (f32[8]{0:T(128)}, f32[8]{0:T(128)S(1)}, u32[]{:S(2)}) copy-start(f32[8]{0:T(128)S(1)} %psum.22) | copy-start | bytes 100
  241.2 79.5 %copy-start.4 = (f32[8,1024]{1,0:T(8,128)}, f32[8,1024]{1,0:T(8,128)S(1)}, u32[]{:S(2)}) copy-start(f32[8,1024]{1,0:T(8,128)S(1)} %get-tuple-element.93) | copy-start | bytes 98308
  259.3 7.3 %copy-start.2 = (bf16[64,1024]{1,0:T(8,128)(2,1)S(1)}, bf16[64,1024]{1,0:T(8,128)(2,1)}, u32[]{:S(2)}) copy-start(bf16[64,1024]{1,0:T(8,128)(2,1)} %param.10) | copy-start | bytes 393220
  266.6 54.1 %copy-start.7 = (f32[8,1024]{1,0:T(8,128)S(1)}, f32[8,1024]{1,0:T(8,128)}, u32[]{:S(2)}) copy-start(f32[8,1024]{1,0:T(8,128)} %param.14) | copy-start | bytes 98308
Sparse Core Ops, SparseCore 0:
  10.2 44.4 all-gather.1
where the time goes:
time: 329 us; the launch traced here: 328 us
  blocking collectives  142 us (43%)
  other arithmetic  83.7 us (25%)
  matrix products  56 us (17%)
  local copies, waits for them, and re-layouts  30.6 us (9%)
  between operations  15 us (5%)
    another operation x3, other arithmetic, precondition(): coeffs = jax.scipy.linalg.cho_solve((chol, True), projection.T)  81 us
    psum x1, blocking collectives, local(): projection = lax.psum(partial_proj, 'rows')  63 us
    psum x1, blocking collectives, local(): curvature = lax.psum(jnp.sum(direction_new * image, axis=1), 'rows')  31.5 us
    psum x1, blocking collectives, local(): inner_new = lax.psum(jnp.sum(precond * residual, axis=1), 'rows')  29.5 us
    another operation x24, local copies, waits for them, and re-layouts  23.1 us
    dot_general x4, matrix products, step_block(): lax.dot_general(block_dirs, kernel_tile, (((1,), (1,)), ((), ())), prefer...  21.8 us
    another operation x30, matrix products, precondition(): coeffs = jax.scipy.linalg.cho_solve((chol, True), projection.T)  20.8 us
    all_gather x1, blocking collectives, local(): lax.all_gather(direction_low, 'rows', axis=1, tiled=True)  18.1 us
  transfers between devices with their start and end apart: 1, of which 0 were waited for; matrix products, arithmetic and copies ran while one was open for 43% of the time, Pallas kernels for 0%

commit v1 on v0

v1 whole, which is shorter than its diff:
```python
import functools
import math

import jax
import jax.numpy as jnp
from jax import lax
from jax.experimental import pallas as pl
from jax.experimental.pallas import tpu as pltpu
from jax.sharding import PartitionSpec as P

HIGH = lax.Precision.HIGHEST
TILE = 128
CHUNK = 256
STORED_BLOCKS = 16


def dot_nn(left, right, precision=None):
    return lax.dot_general(
        left, right, (((1,), (0,)), ((), ())), precision=precision, preferred_element_type=jnp.float32
    )


def dot_nt(left, right, precision=None):
    return lax.dot_general(
        left, right, (((1,), (1,)), ((), ())), precision=precision, preferred_element_type=jnp.float32
    )


def dot_tn(left, right):
    return lax.dot_general(
        left, right, (((0,), (0,)), ((), ())), preferred_element_type=jnp.float32
    )


def norm_rows(features, first):
    wide = features.astype(jnp.float32)
    half = -0.5 * jnp.sum(wide * wide, axis=0, keepdims=True)
    top = half.astype(jnp.bfloat16).astype(jnp.float32)
    rest = half - top
    mid = rest.astype(jnp.bfloat16).astype(jnp.float32)
    low = rest - mid
    row = lax.broadcasted_iota(jnp.int32, (16, features.shape[1]), 0)
    at = 0 if first else 3
    ones = 3 - at
    rows = jnp.where((row >= ones) & (row < ones + 3), 1.0, 0.0)
    rows = jnp.where(row == at, top, rows)
    rows = jnp.where(row == at + 1, mid, rows)
    rows = jnp.where(row == at + 2, low, rows)
    return rows.astype(jnp.bfloat16)


def eye_mask(width):
    shape = (8, width)
    return lax.broadcasted_iota(jnp.int32, shape, 0) == lax.broadcasted_iota(jnp.int32, shape, 1)


def to_row(column, width):
    return jnp.sum(jnp.where(eye_mask(width), column, 0.0), axis=0, keepdims=True)


def to_column(row):
    return jnp.sum(jnp.where(eye_mask(row.shape[1]), row, 0.0), axis=1, keepdims=True)


def kernel(
    n,
    keep,
    points_ref,
    landmarks_ref,
    chol_hbm,
    ridge_ref,
    solution_ref,
    residual_ref,
    direction_ref,
    rz_ref,
    solution_out,
    residual_out,
    direction_out,
    inner_out,
    chol,
    inverse,
    points,
    own_aug,
    col_aug,
    cross_t,
    kernel_store,
    rs_send,
    rs_recv,
    ag,
    proj,
    work,
    inner_buf,
    dirs,
    curv_buf,
    chol_sem,
    rs_sems,
    ag_sems,
    inner_sems,
    dir_sems,
    curv_sems,
    point_recv,
    point_fwd,
    point_side,
    point_back,
):
    me = lax.axis_index("rows")
    feat, local = points_ref.shape
    land = landmarks_ref.shape[1]
    outs = residual_ref.shape[0]
    chips = n // 2
    half = chips // 2
    core = me % 2
    chip = me // 2
    odd = chip % 2
    pos = (1 - odd) * (chip // 2) + odd * (chips - (chip + 1) // 2)
    scale = math.log2(math.e) / feat

    def row_of(position, lane):
        position = (position + chips) % chips
        upper = position // half
        at = (1 - upper) * (2 * position) + upper * (2 * chips - 1 - 2 * position)
        return at * 2 + (core + lane) % 2

    def remote(src, dst, send, recv, to):
        return pltpu.make_async_remote_copy(
            src_ref=src,
            dst_ref=dst,
            send_sem=send,
            recv_sem=recv,
            device_id={"rows": to},
            device_id_type=pl.DeviceIdType.MESH,
        )

    def others(body):
        lax.fori_loop(1, n, lambda k, carry: (body((me + k) % n), carry)[1], 0)

    def send_all(src_of, buf, sems):
        others(lambda to: remote(src_of(to), buf.at[me], sems.at[0, to], sems.at[1, me], to).start())

    def wait_all(src_of, buf, sems):
        others(lambda to: remote(src_of(to), buf.at[to], sems.at[0, to], sems.at[1, to], to).wait_recv())

    def drain(src_of, buf, sems):
        others(lambda to: remote(src_of(to), buf.at[me], sems.at[0, to], sems.at[1, me], to).wait_send())

    chol_copy = pltpu.make_async_copy(chol_hbm, chol, chol_sem)
    chol_copy.start()

    barrier = pltpu.get_barrier_semaphore()
    others(lambda to: pl.semaphore_signal(
        barrier, inc=1, device_id={"rows": to}, device_id_type=pl.DeviceIdType.MESH))
    pl.semaphore_wait(barrier, n - 1)

    right = row_of(pos + 1, 0)
    left = row_of(pos - 1, 0)
    partner = row_of(pos, 1)
    own_slot = points.at[me]
    first_right = remote(points_ref, own_slot, point_fwd.at[me], point_recv.at[me], right)
    first_left = remote(points_ref, own_slot, point_back, point_recv.at[me], left)
    first_side = remote(points_ref, own_slot, point_side.at[me], point_recv.at[me], partner)
    first_right.start()
    first_left.start()
    first_side.start()

    own_aug[0:feat, :] = points_ref[...]
    own_aug[feat:, :] = norm_rows(points_ref[...], True)
    col_aug[0:feat, :] = landmarks_ref[...]
    col_aug[feat:, :] = norm_rows(landmarks_ref[...], False)

    def entries(left_aug, at, right_aug):
        return jnp.exp2(dot_tn(left_aug[:, pl.ds(at, CHUNK)], right_aug[...]) * scale)

    proj[...] = jnp.zeros_like(proj)

    def project(i, carry):
        at = pl.multiple_of(i * CHUNK, CHUNK)
        proj[...] += dot_nn(residual_ref[:, pl.ds(at, CHUNK)], entries(own_aug, at, col_aug), HIGH)
        return carry

    lax.fori_loop(0, local // CHUNK, project, 0)

    tiles = land // TILE
    rows_per = outs * tiles // n
    for piece in range(n):
        h, j = piece // tiles, piece % tiles
        rs_send[piece] = proj[h * rows_per:(h + 1) * rows_per, j * TILE:(j + 1) * TILE]
    send_all(lambda to: rs_send.at[to], rs_recv, rs_sems)
    rs_recv[me] = rs_send[me]

    def landmark_rows(i, carry):
        at = pl.multiple_of(i * CHUNK, CHUNK)
        cross_t[pl.ds(at, CHUNK), :] = entries(col_aug, at, own_aug)
        return carry

    lax.fori_loop(0, land // CHUNK, landmark_rows, 0)

    def make_block(owner, slot):
        col_aug[0:feat, :] = points[owner]
        col_aug[feat:, :] = norm_rows(points[owner], False)

        def step(i, carry):
            at = pl.multiple_of(i * CHUNK, CHUNK)
            kernel_store[slot, pl.ds(at, CHUNK), :] = entries(col_aug, at, own_aug).astype(jnp.bfloat16)
            return carry

        lax.fori_loop(0, local // CHUNK, step, 0)

    own_points = pltpu.make_async_copy(points_ref, own_slot, chol_sem)
    chol_copy.wait()
    own_points.start()
    own_points.wait()

    row = lax.broadcasted_iota(jnp.int32, (TILE, TILE), 0)
    col = lax.broadcasted_iota(jnp.int32, (TILE, TILE), 1)

    blocks = [chol[b * TILE:(b + 1) * TILE, b * TILE:(b + 1) * TILE] for b in range(tiles)]
    for b in range(tiles):
        inverse[b] = jnp.where(row == col, 1.0 / blocks[b], 0.0)
    size = 1
    while size < TILE:
        below = (row // size == col // size + 1) & (row // (2 * size) == col // (2 * size))
        for b in range(tiles):
            off = jnp.where(below, chol[b * TILE:(b + 1) * TILE, b * TILE:(b + 1) * TILE], 0.0)
            if size == 1:
                on_row = jnp.sum(inverse[b], axis=1, keepdims=True)
                on_col = jnp.sum(inverse[b], axis=0, keepdims=True)
                change = on_row * off * on_col
            else:
                change = dot_nn(dot_nn(inverse[b], off, HIGH), inverse[b], HIGH)
            inverse[b] = inverse[b] - change
        size *= 2

    wait_all(lambda to: rs_send.at[to], rs_recv, rs_sems)
    ag[me] = jnp.sum(rs_recv[...], axis=0)
    send_all(lambda to: ag.at[me], ag, ag_sems)

    if keep:
        make_block(me, me)

    def relay(s, both):
        near = row_of(pos - s, 0)
        remote(points_ref, points.at[near], point_fwd.at[near], point_recv.at[near], right).wait_recv()
        if both:
            remote(points.at[near], points.at[near], point_fwd.at[near], point_recv.at[near], right).start()
        remote(points.at[near], points.at[near], point_side.at[near], point_recv.at[near], partner).start()
        if both:
            far = row_of(pos + s, 0)
            remote(points_ref, points.at[far], point_fwd.at[far], point_recv.at[far], left).wait_recv()
            remote(points.at[far], points.at[far], point_side.at[far], point_recv.at[far], partner).start()

            @pl.when(s < half - 1)
            def _():
                remote(points.at[far], points.at[far], point_fwd.at[far], point_recv.at[far], left).start()

        def build(lane):
            def one(way, carry):
                owner = row_of(pos - s + 2 * s * way, lane)
                if lane == 1:
                    remote(points_ref, points.at[owner], point_side.at[owner], point_recv.at[owner], partner).wait_recv()
                if keep:
                    make_block(owner, owner)
                return carry

            lax.fori_loop(0, 2 if both else 1, one, 0)

        build(0)
        build(1)

    relay(1, True)
    remote(points_ref, points.at[partner], point_side.at[partner], point_recv.at[partner], partner).wait_recv()

    wait_all(lambda to: ag.at[me], ag, ag_sems)
    for piece in range(n):
        h, j = piece // tiles, piece % tiles
        work[h * rows_per:(h + 1) * rows_per, j * TILE:(j + 1) * TILE] = ag[piece]
    for b in range(tiles):
        at, end = b * TILE, (b + 1) * TILE
        solved = dot_nt(work[:, at:end], inverse[b], HIGH)
        work[:, at:end] = solved
        if end < land:
            work[:, end:] -= dot_nt(solved, chol[end:, at:end], HIGH)
    for b in reversed(range(tiles)):
        at, end = b * TILE, (b + 1) * TILE
        solved = dot_nn(work[:, at:end], inverse[b], HIGH)
        work[:, at:end] = solved
        if at > 0:
            work[:, :at] -= dot_nn(solved, chol[at:end, :at], HIGH)

    ridge = ridge_ref[0]
    residual = residual_ref[...]
    precond = (residual - dot_nn(work[...], cross_t[...], HIGH)) / ridge
    inner_buf[me] = to_row(jnp.sum(precond * residual, axis=1, keepdims=True), TILE)
    send_all(lambda to: inner_buf.at[me], inner_buf, inner_sems)

    if keep:
        make_block(partner, partner)
    lax.fori_loop(2, min(3, half), lambda s, carry: (relay(s, True), carry)[1], 0)
    wait_all(lambda to: inner_buf.at[me], inner_buf, inner_sems)
    inner_row = jnp.sum(inner_buf[...], axis=0)
    inner_out[...] = inner_row[:, :outs]
    inner = to_column(inner_row)
    direction_new = precond + (inner / to_column(rz_ref[...])) * direction_ref[...]
    direction_out[...] = direction_new
    dirs[me] = direction_new.astype(jnp.bfloat16)
    send_all(lambda to: dirs.at[me], dirs, dir_sems)

    lax.fori_loop(3, half, lambda s, carry: (relay(s, True), carry)[1], 0)
    relay(half, False)

    def image_part(owner, slot):
        if not keep:
            make_block(owner, slot)
        proj[...] += dot_nn(dirs[owner], kernel_store[slot])

    proj[...] = jnp.zeros_like(proj)
    image_part(me, me if keep else 0)

    def gather_image(to):
        remote(dirs.at[me], dirs.at[to], dir_sems.at[0, to], dir_sems.at[1, to], to).wait_recv()
        image_part(to, to if keep else 0)

    others(gather_image)

    direction_new = direction_out[...]
    image = proj[...] + ridge * direction_new
    curv_buf[me] = to_row(jnp.sum(direction_new * image, axis=1, keepdims=True), TILE)
    send_all(lambda to: curv_buf.at[me], curv_buf, curv_sems)

    drain(lambda to: rs_send.at[to], rs_recv, rs_sems)
    drain(lambda to: ag.at[me], ag, ag_sems)
    drain(lambda to: inner_buf.at[me], inner_buf, inner_sems)
    drain(lambda to: dirs.at[me], dirs, dir_sems)
    first_right.wait_send()
    first_left.wait_send()
    first_side.wait_send()

    def relay_drain(s, both):
        near = row_of(pos - s, 0)
        remote(points.at[near], points.at[near], point_side.at[near], point_recv.at[near], partner).wait_send()
        if both:
            remote(points.at[near], points.at[near], point_fwd.at[near], point_recv.at[near], right).wait_send()
            far = row_of(pos + s, 0)
            remote(points.at[far], points.at[far], point_side.at[far], point_recv.at[far], partner).wait_send()

            @pl.when(s < half - 1)
            def _():
                remote(points.at[far], points.at[far], point_fwd.at[far], point_recv.at[far], left).wait_send()

    lax.fori_loop(1, half, lambda s, carry: (relay_drain(s, True), carry)[1], 0)
    relay_drain(half, False)

    wait_all(lambda to: curv_buf.at[me], curv_buf, curv_sems)
    alpha = to_column(inner_out[...] / jnp.sum(curv_buf[...], axis=0)[:, :outs])
    solution_out[...] = solution_ref[...] + alpha * direction_new
    residual_out[...] = residual_ref[...] - alpha * image
    drain(lambda to: curv_buf.at[me], curv_buf, curv_sems)


def solution(mesh):
    n = mesh.shape["rows"]

    def local(points, landmarks, chol, ridge, solution, residual, direction, rz_prev):
        feat, own = points.shape
        land = landmarks.shape[1]
        outs = residual.shape[0]
        keep = n <= STORED_BLOCKS
        piece = outs * land // (TILE * n)
        f32, bf16 = jnp.float32, jnp.bfloat16
        vmem = pl.BlockSpec(memory_space=pltpu.VMEM)
        wide = jax.ShapeDtypeStruct((outs, own), f32)
        dma = pltpu.SemaphoreType.DMA
        results = pl.pallas_call(
            functools.partial(kernel, n, keep),
            out_shape=(wide, wide, wide, jax.ShapeDtypeStruct((1, outs), f32)),
            in_specs=[
                vmem,
                vmem,
                pl.BlockSpec(memory_space=pl.ANY),
                pl.BlockSpec(memory_space=pltpu.SMEM),
                vmem,
                vmem,
                vmem,
                vmem,
            ],
            out_specs=(vmem,) * 4,
            scratch_shapes=[
                pltpu.VMEM((land, land), f32),
                pltpu.VMEM((land // TILE, TILE, TILE), f32),
                pltpu.VMEM((n, feat, own), bf16),
                pltpu.VMEM((feat + 16, own), bf16),
                pltpu.VMEM((feat + 16, own), bf16),
                pltpu.VMEM((land, own), f32),
                pltpu.VMEM((n if keep else 1, own, own), bf16),
                pltpu.VMEM((n, piece, TILE), f32),
                pltpu.VMEM((n, piece, TILE), f32),
                pltpu.VMEM((n, piece, TILE), f32),
                pltpu.VMEM((outs, land), f32),
                pltpu.VMEM((outs, land), f32),
                pltpu.VMEM((n, 1, TILE), f32),
                pltpu.VMEM((n, outs, own), bf16),
                pltpu.VMEM((n, 1, TILE), f32),
                dma,
                dma((2, n)),
                dma((2, n)),
                dma((2, n)),
                dma((2, n)),
                dma((2, n)),
                dma((n,)),
                dma((n,)),
                dma((n,)),
                dma,
            ],
            compiler_params=pltpu.CompilerParams(
                collective_id=0, has_side_effects=True, vmem_limit_bytes=62 * 1024 * 1024
            ),
            name="cg_step",
        )(points, landmarks, chol, ridge, solution, residual, direction, rz_prev.reshape(1, outs))
        return (results[0], results[1], results[2], results[3].reshape(outs))

    wide_spec = P(None, ("groups", "rows"))
    in_specs = (
        wide_spec,
        P(None, "groups"),
        P("groups", None),
        P("groups"),
        wide_spec,
        wide_spec,
        wide_spec,
        P("groups"),
    )
    out_specs = (wide_spec, wide_spec, wide_spec, P("groups"))
    return jax.shard_map(local, mesh=mesh, in_specs=in_specs, out_specs=out_specs, check_vma=False)
```

time: 329 us -> 74.2 us (0.23)
  blocking collectives: 142 us -> 0 us
  other arithmetic: 83.7 us -> 0 us
  Pallas kernels: 0 us -> 67.2 us
  matrix products: 56 us -> 0 us
  local copies, waits for them, and re-layouts: 30.6 us -> 5.31 us
  between operations: 15 us -> 1.29 us
    psum x3 -> x0, blocking collectives: 124 us -> none  [the longest x1 63 us: local(): projection = lax.psum(partial_proj, 'rows')]
    another operation x3 -> x0, other arithmetic: 81 us -> none  [precondition(): coeffs = jax.scipy.linalg.cho_solve((chol, True), projection.T)]
    pallas_call x0 -> x1, Pallas kernels: none -> 67.2 us  [local(): pl.pallas_call(functools.partial(kernel, n, keep), out_shape=(wide, wide,...]
    dot_general x7 -> x0, matrix products: 35.2 us -> none  [the longest x4 21.8 us: step_block(): lax.dot_general(block_dirs, kernel_tile, (((1,), (1,)), ((), ())), prefer...]
    another operation x29 -> x0, local copies, waits for them, and re-layouts: 23.1 us -> none
    another operation x30 -> x0, matrix products: 20.8 us -> none  [precondition(): coeffs = jax.scipy.linalg.cho_solve((chol, True), projection.T)]
    all_gather x1 -> x0, blocking collectives: 18.1 us -> none  [local(): lax.all_gather(direction_low, 'rows', axis=1, tiled=True)]
    reshape x1 -> x0, local copies, waits for them, and re-layouts: 4.5 us -> none  [split_blocks(): values.reshape(values.shape[:-1] + (blocks, block_len))]
  transfers between devices with their start and end apart: 1 -> 0, of which waited for: 0 -> 0; matrix products, arithmetic and copies ran while one was open for 43% -> 0% of each run, Pallas kernels for 0% -> 0%
where the time goes in v1:
time: 74.2 us; the launch traced here: 73.8 us
  Pallas kernels  67.2 us (91%)
  local copies, waits for them, and re-layouts  5.31 us (7%)
  between operations  1.29 us (2%)
    pallas_call x1, Pallas kernels, local(): pl.pallas_call(functools.partial(kernel, n, keep), out_shape=(wide, wide,...  67.2 us
    unnamed x4, local copies, waits for them, and re-layouts  5.31 us

profile of v1, /device:TPU:0, one launch (start us, length us, event | category | flops | bytes accessed | tf_op | source)
XLA Modules:
  0.0 73.8 jit_solution(432551320504240890)
XLA Ops:
  1.3 67.2 %cg_step.1 = (f32[8,1024]{1,0:T(8,128)}, f32[8,1024]{1,0:T(8,128)}, f32[8,1024]{1,0:T(8,128)}, f32[1,8]{1,0:T(1,128)}) custom-call(bf16[64,1024]{1,0:T(8,128)(2,1)} %points_ref.1, bf16[64,1024]{1,0:T(8,128)(2,1)} %landmarks_ref.1, f32[1024,1024]{1,0:T(8,128)} %chol_hbm.1, f32[1]{0:T(128)S(6)} %copy.16.ridge_ref, f32[8,1024]{1,0:T(8,128)} %solution_ref.1, ...), custom_call_target="tpu_custom_call" | custom-call | tf_op jit(solution)/shard_map/cg_step/pallas_call | solution.py:372
  68.5 1.4 %copy.17 = f32[8,1024]{1,0:T(8,128)} copy(f32[8,1024]{1,0:T(8,128)} %get-tuple-element.16) | data formatting | bytes 65536
  69.9 1.4 %copy.18 = f32[8,1024]{1,0:T(8,128)} copy(f32[8,1024]{1,0:T(8,128)} %get-tuple-element.17) | data formatting | bytes 65536
  71.3 1.4 %copy.19 = f32[8,1024]{1,0:T(8,128)} copy(f32[8,1024]{1,0:T(8,128)} %get-tuple-element.18) | data formatting | bytes 65536
  72.6 1.2 %copy.20 = f32[8]{0:T(128)} copy(f32[8]{0:T(128)} %bitcast.3) | data formatting | bytes 64

commit v2 on v1

--- a/solution.py
+++ b/solution.py
@@ -11,6 +11,7 @@
 HIGH = lax.Precision.HIGHEST
 TILE = 128
 CHUNK = 256
+GROUP = 2 * TILE
 STORED_BLOCKS = 16
 
 
@@ -30,6 +31,28 @@
     return lax.dot_general(
         left, right, (((0,), (0,)), ((), ())), preferred_element_type=jnp.float32
     )
+
+
+def split(values):
+    top = values.astype(jnp.bfloat16).astype(jnp.float32)
+    rest = values - top
+    mid = rest.astype(jnp.bfloat16).astype(jnp.float32)
+    return top, mid, rest - mid
+
+
+def store_split(ref, at, values):
+    for term, part in enumerate(split(values)):
+        ref[(term,) + at] = part.astype(jnp.bfloat16)
+
+
+def dot_split(left, parts, dot):
+    outs = left.shape[0]
+    stacked = jnp.concatenate(split(left), axis=0).astype(jnp.bfloat16)
+    high = dot(stacked, parts[0])
+    mid = dot(stacked[:2 * outs], parts[1])
+    low = dot(stacked[:2 * outs], parts[2])
+    small = low[:outs] + mid[outs:] + high[2 * outs:]
+    return high[:outs] + (high[outs:2 * outs] + mid[:outs] + small)
 
 
 def norm_rows(features, first):
@@ -69,15 +92,16 @@
     landmarks_ref,
     chol_hbm,
     ridge_ref,
-    solution_ref,
     residual_ref,
     direction_ref,
     rz_ref,
-    solution_out,
-    residual_out,
+    image_out,
     direction_out,
     inner_out,
+    alpha_out,
     chol,
+    chol_parts,
+    inverse_parts,
     inverse,
     points,
     own_aug,
@@ -149,7 +173,6 @@
     barrier = pltpu.get_barrier_semaphore()
     others(lambda to: pl.semaphore_signal(
         barrier, inc=1, device_id={"rows": to}, device_id_type=pl.DeviceIdType.MESH))
-    pl.semaphore_wait(barrier, n - 1)
 
     right = row_of(pos + 1, 0)
     left = row_of(pos - 1, 0)
@@ -158,9 +181,6 @@
     first_right = remote(points_ref, own_slot, point_fwd.at[me], point_recv.at[me], right)
     first_left = remote(points_ref, own_slot, point_back, point_recv.at[me], left)
     first_side = remote(points_ref, own_slot, point_side.at[me], point_recv.at[me], partner)
-    first_right.start()
-    first_left.start()
-    first_side.start()
 
     own_aug[0:feat, :] = points_ref[...]
     own_aug[feat:, :] = norm_rows(points_ref[...], True)
@@ -174,22 +194,29 @@
 
     def project(i, carry):
         at = pl.multiple_of(i * CHUNK, CHUNK)
-        proj[...] += dot_nn(residual_ref[:, pl.ds(at, CHUNK)], entries(own_aug, at, col_aug), HIGH)
+        parts = [part.astype(jnp.bfloat16) for part in split(entries(own_aug, at, col_aug))]
+        proj[...] += dot_split(residual_ref[:, pl.ds(at, CHUNK)], parts, dot_nn)
         return carry
 
     lax.fori_loop(0, local // CHUNK, project, 0)
 
+    pl.semaphore_wait(barrier, n - 1)
+
     tiles = land // TILE
+    groups = land // GROUP
     rows_per = outs * tiles // n
     for piece in range(n):
         h, j = piece // tiles, piece % tiles
         rs_send[piece] = proj[h * rows_per:(h + 1) * rows_per, j * TILE:(j + 1) * TILE]
     send_all(lambda to: rs_send.at[to], rs_recv, rs_sems)
     rs_recv[me] = rs_send[me]
+    first_right.start()
+    first_left.start()
+    first_side.start()
 
     def landmark_rows(i, carry):
         at = pl.multiple_of(i * CHUNK, CHUNK)
-        cross_t[pl.ds(at, CHUNK), :] = entries(col_aug, at, own_aug)
+        store_split(cross_t, (pl.ds(at, CHUNK), slice(None)), entries(col_aug, at, own_aug))
         return carry
 
     lax.fori_loop(0, land // CHUNK, landmark_rows, 0)
@@ -229,6 +256,18 @@
                 change = dot_nn(dot_nn(inverse[b], off, HIGH), inverse[b], HIGH)
             inverse[b] = inverse[b] - change
         size *= 2
+    for b in range(groups):
+        upper, lower = inverse[2 * b], inverse[2 * b + 1]
+        at, end = b * GROUP, (b + 1) * GROUP
+        off = chol[at + TILE:end, at:at + TILE]
+        change = dot_nn(dot_nn(lower, off, HIGH), upper, HIGH)
+        zero = jnp.zeros_like(upper)
+        whole = jnp.concatenate(
+            [jnp.concatenate([upper, zero], axis=1), jnp.concatenate([-change, lower], axis=1)], axis=0
+        )
+        store_split(inverse_parts, (b,), whole)
+        if b > 0:
+            store_split(chol_parts, (slice(at, end), slice(0, at)), chol[at:end, :at])
 
     wait_all(lambda to: rs_send.at[to], rs_recv, rs_sems)
     ag[me] = jnp.sum(rs_recv[...], axis=0)
@@ -273,22 +312,28 @@
     for piece in range(n):
         h, j = piece // tiles, piece % tiles
         work[h * rows_per:(h + 1) * rows_per, j * TILE:(j + 1) * TILE] = ag[piece]
-    for b in range(tiles):
-        at, end = b * TILE, (b + 1) * TILE
-        solved = dot_nt(work[:, at:end], inverse[b], HIGH)
-        work[:, at:end] = solved
-        if end < land:
-            work[:, end:] -= dot_nt(solved, chol[end:, at:end], HIGH)
-    for b in reversed(range(tiles)):
-        at, end = b * TILE, (b + 1) * TILE
-        solved = dot_nn(work[:, at:end], inverse[b], HIGH)
-        work[:, at:end] = solved
-        if at > 0:
-            work[:, :at] -= dot_nn(solved, chol[at:end, :at], HIGH)
+    pieces = [work[:, b * GROUP:(b + 1) * GROUP] for b in range(groups)]
+
+    def block_parts(i, j):
+        rows, cols = slice(i * GROUP, (i + 1) * GROUP), slice(j * GROUP, (j + 1) * GROUP)
+        return [chol_parts[term, rows, cols] for term in range(3)]
+
+    def inverse_of(b):
+        return [inverse_parts[term, b] for term in range(3)]
+
+    for b in range(groups):
+        pieces[b] = dot_split(pieces[b], inverse_of(b), dot_nt)
+        for i in range(b + 1, groups):
+            pieces[i] = pieces[i] - dot_split(pieces[b], block_parts(i, b), dot_nt)
+    for b in reversed(range(groups)):
+        pieces[b] = dot_split(pieces[b], inverse_of(b), dot_nn)
+        for j in reversed(range(b)):
+            pieces[j] = pieces[j] - dot_split(pieces[b], block_parts(b, j), dot_nn)
+    coeffs = jnp.concatenate(pieces, axis=1)
 
     ridge = ridge_ref[0]
     residual = residual_ref[...]
-    precond = (residual - dot_nn(work[...], cross_t[...], HIGH)) / ridge
+    precond = (residual - dot_split(coeffs, [cross_t.at[term][...] for term in range(3)], dot_nn)) / ridge
     inner_buf[me] = to_row(jnp.sum(precond * residual, axis=1, keepdims=True), TILE)
     send_all(lambda to: inner_buf.at[me], inner_buf, inner_sems)
 
@@ -323,6 +368,7 @@
 
     direction_new = direction_out[...]
     image = proj[...] + ridge * direction_new
+    image_out[...] = image
     curv_buf[me] = to_row(jnp.sum(direction_new * image, axis=1, keepdims=True), TILE)
     send_all(lambda to: curv_buf.at[me], curv_buf, curv_sems)
 
@@ -350,10 +396,28 @@
     relay_drain(half, False)
 
     wait_all(lambda to: curv_buf.at[me], curv_buf, curv_sems)
-    alpha = to_column(inner_out[...] / jnp.sum(curv_buf[...], axis=0)[:, :outs])
-    solution_out[...] = solution_ref[...] + alpha * direction_new
-    residual_out[...] = residual_ref[...] - alpha * image
+    alpha_out[...] = inner_out[...] / jnp.sum(curv_buf[...], axis=0)[:, :outs]
     drain(lambda to: curv_buf.at[me], curv_buf, curv_sems)
+
+
+def finish(
+    image_ref,
+    direction_ref,
+    inner_ref,
+    alpha_ref,
+    solution_ref,
+    residual_ref,
+    solution_out,
+    residual_out,
+    direction_out,
+    inner_out,
+):
+    alpha = to_column(alpha_ref[...])
+    direction = direction_ref[...]
+    solution_out[...] = solution_ref[...] + alpha * direction
+    residual_out[...] = residual_ref[...] - alpha * image_ref[...]
+    direction_out[...] = direction
+    inner_out[...] = inner_ref[...]
 
 
 def solution(mesh):
@@ -368,10 +432,11 @@
         f32, bf16 = jnp.float32, jnp.bfloat16
         vmem = pl.BlockSpec(memory_space=pltpu.VMEM)
         wide = jax.ShapeDtypeStruct((outs, own), f32)
+        thin = jax.ShapeDtypeStruct((1, outs), f32)
         dma = pltpu.SemaphoreType.DMA
         results = pl.pallas_call(
             functools.partial(kernel, n, keep),
-            out_shape=(wide, wide, wide, jax.ShapeDtypeStruct((1, outs), f32)),
+            out_shape=(wide, wide, thin, thin),
             in_specs=[
                 vmem,
                 vmem,
@@ -380,16 +445,17 @@
                 vmem,
                 vmem,
                 vmem,
-                vmem,
             ],
             out_specs=(vmem,) * 4,
             scratch_shapes=[
                 pltpu.VMEM((land, land), f32),
+                pltpu.VMEM((3, land, land), bf16),
+                pltpu.VMEM((3, land // GROUP, GROUP, GROUP), bf16),
                 pltpu.VMEM((land // TILE, TILE, TILE), f32),
                 pltpu.VMEM((n, feat, own), bf16),
                 pltpu.VMEM((feat + 16, own), bf16),
                 pltpu.VMEM((feat + 16, own), bf16),
-                pltpu.VMEM((land, own), f32),
+                pltpu.VMEM((3, land, own), bf16),
                 pltpu.VMEM((n if keep else 1, own, own), bf16),
                 pltpu.VMEM((n, piece, TILE), f32),
                 pltpu.VMEM((n, piece, TILE), f32),
@@ -414,7 +480,14 @@
                 collective_id=0, has_side_effects=True, vmem_limit_bytes=62 * 1024 * 1024
             ),
             name="cg_step",
-        )(points, landmarks, chol, ridge, solution, residual, direction, rz_prev.reshape(1, outs))
+        )(points, landmarks, chol, ridge, residual, direction, rz_prev.reshape(1, outs))
+        results = pl.pallas_call(
+            finish,
+            out_shape=(wide, wide, wide, thin),
+            in_specs=[vmem] * 6,
+            out_specs=(vmem,) * 4,
+            name="finish",
+        )(*results, solution, residual)
         return (results[0], results[1], results[2], results[3].reshape(outs))
 
     wide_spec = P(None, ("groups", "rows"))

time: 74.2 us -> 62.7 us (0.85)
  Pallas kernels: 67.2 us -> 61.2 us
  local copies, waits for them, and re-layouts: 5.31 us -> 0 us
    pallas_call x1, Pallas kernels: 67.2 us -> 59.7 us  [local(): pl.pallas_call(functools.partial(kernel, n, keep), out_shape=(wide, wide,...]
    unnamed x4 -> x0, local copies, waits for them, and re-layouts: 5.31 us -> none
    pallas_call x0 -> x1, Pallas kernels: none -> 1.54 us  [local(): pl.pallas_call(finish, out_shape=(wide, wide, wide, thin), in_specs=[vmem...]
where the time goes in v2:
time: 62.7 us; the launch traced here: 62.5 us
  Pallas kernels  61.2 us (98%)
  between operations  1.29 us (2%)
    pallas_call x1, Pallas kernels, local(): pl.pallas_call(functools.partial(kernel, n, keep), out_shape=(wide, wide,...  59.7 us
    pallas_call x1, Pallas kernels, local(): pl.pallas_call(finish, out_shape=(wide, wide, wide, thin), in_specs=[vmem...  1.54 us

profile of v2, /device:TPU:0, one launch (start us, length us, event | category | flops | bytes accessed | tf_op | source)
XLA Modules:
  0.0 62.5 jit_solution(2749040080665586787)
XLA Ops:
  1.3 59.7 %cg_step.1 = (f32[8,1024]{1,0:T(8,128)}, f32[8,1024]{1,0:T(8,128)}, f32[1,8]{1,0:T(1,128)}, f32[1,8]{1,0:T(1,128)}) custom-call(bf16[64,1024]{1,0:T(8,128)(2,1)} %points_ref.1, bf16[64,1024]{1,0:T(8,128)(2,1)} %landmarks_ref.1, f32[1024,1024]{1,0:T(8,128)} %chol_hbm.1, f32[1]{0:T(128)S(6)} %copy.12.ridge_ref, f32[8,1024]{1,0:T(8,128)} %residual_ref.3, ...), custom_call_target="tpu_custom_call" | custom-call | tf_op jit(solution)/shard_map/cg_step/pallas_call | solution.py:437
  60.9 1.5 %finish.1 = (f32[8,1024]{1,0:T(8,128)}, f32[8,1024]{1,0:T(8,128)}, f32[8,1024]{1,0:T(8,128)}, f32[1,8]{1,0:T(1,128)}) custom-call(f32[8,1024]{1,0:T(8,128)} %get-tuple-element.12.image_ref, f32[8,1024]{1,0:T(8,128)} %get-tuple-element.13.direction_ref, f32[1,8]{1,0:T(1,128)} %get-tuple-element.14.inner_ref, f32[1,8]{1,0:T(1,128)} %get-tuple-element.15.alpha_ref, ...), custom_call_target="tpu_custom_call" | custom-call | tf_op jit(solution)/shard_map/finish/pallas_call | solution.py:484

commit v3 on v2

--- a/solution.py
+++ b/solution.py
@@ -126,6 +126,7 @@
     point_fwd,
     point_side,
     point_back,
+    share_sems,
 ):
     me = lax.axis_index("rows")
     feat, local = points_ref.shape
@@ -225,12 +226,8 @@
         col_aug[0:feat, :] = points[owner]
         col_aug[feat:, :] = norm_rows(points[owner], False)
 
-        def step(i, carry):
-            at = pl.multiple_of(i * CHUNK, CHUNK)
-            kernel_store[slot, pl.ds(at, CHUNK), :] = entries(col_aug, at, own_aug).astype(jnp.bfloat16)
-            return carry
-
-        lax.fori_loop(0, local // CHUNK, step, 0)
+        for at in range(0, local, CHUNK):
+            kernel_store[slot, at:at + CHUNK, :] = entries(col_aug, at, own_aug).astype(jnp.bfloat16)
 
     own_points = pltpu.make_async_copy(points_ref, own_slot, chol_sem)
     chol_copy.wait()
@@ -240,22 +237,75 @@
     row = lax.broadcasted_iota(jnp.int32, (TILE, TILE), 0)
     col = lax.broadcasted_iota(jnp.int32, (TILE, TILE), 1)
 
-    blocks = [chol[b * TILE:(b + 1) * TILE, b * TILE:(b + 1) * TILE] for b in range(tiles)]
-    for b in range(tiles):
-        inverse[b] = jnp.where(row == col, 1.0 / blocks[b], 0.0)
+    share = tiles // 2
+    first = core * share
+
+    def own_block(b):
+        at = pl.multiple_of((first + b) * TILE, TILE)
+        return chol[pl.ds(at, TILE), pl.ds(at, TILE)]
+
+    inverted = [jnp.where(row == col, 1.0 / own_block(b), 0.0) for b in range(share)]
     size = 1
     while size < TILE:
         below = (row // size == col // size + 1) & (row // (2 * size) == col // (2 * size))
-        for b in range(tiles):
-            off = jnp.where(below, chol[b * TILE:(b + 1) * TILE, b * TILE:(b + 1) * TILE], 0.0)
+        for b in range(share):
+            off = jnp.where(below, own_block(b), 0.0)
             if size == 1:
-                on_row = jnp.sum(inverse[b], axis=1, keepdims=True)
-                on_col = jnp.sum(inverse[b], axis=0, keepdims=True)
+                on_row = jnp.sum(inverted[b], axis=1, keepdims=True)
+                on_col = jnp.sum(inverted[b], axis=0, keepdims=True)
                 change = on_row * off * on_col
             else:
-                change = dot_nn(dot_nn(inverse[b], off, HIGH), inverse[b], HIGH)
-            inverse[b] = inverse[b] - change
+                change = dot_nn(dot_nn(inverted[b], off, HIGH), inverted[b], HIGH)
+            inverted[b] = inverted[b] - change
         size *= 2
+    for b in range(share):
+        inverse[first + b] = inverted[b]
+
+    wait_all(lambda to: rs_send.at[to], rs_recv, rs_sems)
+    ag[me] = jnp.sum(rs_recv[...], axis=0)
+    send_all(lambda to: ag.at[me], ag, ag_sems)
+
+    shares = inverse.at[pl.ds(first, share)]
+    shared = remote(shares, shares, share_sems.at[0], share_sems.at[1], partner)
+    shared.start()
+
+    if keep:
+        make_block(me, me)
+
+    def relay(s, both):
+        near = row_of(pos - s, 0)
+        remote(points_ref, points.at[near], point_fwd.at[near], point_recv.at[near], right).wait_recv()
+        if both:
+            remote(points.at[near], points.at[near], point_fwd.at[near], point_recv.at[near], right).start()
+        remote(points.at[near], points.at[near], point_side.at[near], point_recv.at[near], partner).start()
+        if both:
+            far = row_of(pos + s, 0)
+            remote(points_ref, points.at[far], point_fwd.at[far], point_recv.at[far], left).wait_recv()
+            remote(points.at[far], points.at[far], point_side.at[far], point_recv.at[far], partner).start()
+
+            @pl.when(s < half - 1)
+            def _():
+                remote(points.at[far], points.at[far], point_fwd.at[far], point_recv.at[far], left).start()
+
+        def build(lane):
+            def one(way, carry):
+                owner = row_of(pos - s + 2 * s * way, lane)
+                if lane == 1:
+                    remote(points_ref, points.at[owner], point_side.at[owner], point_recv.at[owner], partner).wait_recv()
+                if keep:
+                    make_block(owner, owner)
+                return carry
+
+            lax.fori_loop(0, 2 if both else 1, one, 0)
+
+        build(0)
+        build(1)
+
+    relay(1, True)
+    remote(points_ref, points.at[partner], point_side.at[partner], point_recv.at[partner], partner).wait_recv()
+
+    other = inverse.at[pl.ds(share - first, share)]
+    remote(other, other, share_sems.at[0], share_sems.at[1], partner).wait_recv()
     for b in range(groups):
         upper, lower = inverse[2 * b], inverse[2 * b + 1]
         at, end = b * GROUP, (b + 1) * GROUP
@@ -269,45 +319,6 @@
         if b > 0:
             store_split(chol_parts, (slice(at, end), slice(0, at)), chol[at:end, :at])
 
-    wait_all(lambda to: rs_send.at[to], rs_recv, rs_sems)
-    ag[me] = jnp.sum(rs_recv[...], axis=0)
-    send_all(lambda to: ag.at[me], ag, ag_sems)
-
-    if keep:
-        make_block(me, me)
-
-    def relay(s, both):
-        near = row_of(pos - s, 0)
-        remote(points_ref, points.at[near], point_fwd.at[near], point_recv.at[near], right).wait_recv()
-        if both:
-            remote(points.at[near], points.at[near], point_fwd.at[near], point_recv.at[near], right).start()
-        remote(points.at[near], points.at[near], point_side.at[near], point_recv.at[near], partner).start()
-        if both:
-            far = row_of(pos + s, 0)
-            remote(points_ref, points.at[far], point_fwd.at[far], point_recv.at[far], left).wait_recv()
-            remote(points.at[far], points.at[far], point_side.at[far], point_recv.at[far], partner).start()
-
-            @pl.when(s < half - 1)
-            def _():
-                remote(points.at[far], points.at[far], point_fwd.at[far], point_recv.at[far], left).start()
-
-        def build(lane):
-            def one(way, carry):
-                owner = row_of(pos - s + 2 * s * way, lane)
-                if lane == 1:
-                    remote(points_ref, points.at[owner], point_side.at[owner], point_recv.at[owner], partner).wait_recv()
-                if keep:
-                    make_block(owner, owner)
-                return carry
-
-            lax.fori_loop(0, 2 if both else 1, one, 0)
-
-        build(0)
-        build(1)
-
-    relay(1, True)
-    remote(points_ref, points.at[partner], point_side.at[partner], point_recv.at[partner], partner).wait_recv()
-
     wait_all(lambda to: ag.at[me], ag, ag_sems)
     for piece in range(n):
         h, j = piece // tiles, piece % tiles
@@ -376,6 +387,7 @@
     drain(lambda to: ag.at[me], ag, ag_sems)
     drain(lambda to: inner_buf.at[me], inner_buf, inner_sems)
     drain(lambda to: dirs.at[me], dirs, dir_sems)
+    shared.wait_send()
     first_right.wait_send()
     first_left.wait_send()
     first_side.wait_send()
@@ -475,6 +487,7 @@
                 dma((n,)),
                 dma((n,)),
                 dma,
+                dma((2,)),
             ],
             compiler_params=pltpu.CompilerParams(
                 collective_id=0, has_side_effects=True, vmem_limit_bytes=62 * 1024 * 1024

time: 62.7 us -> 53.1 us (0.85)
  Pallas kernels: 61.2 us -> 51.6 us
    pallas_call x1, Pallas kernels: 59.7 us -> 50.1 us  [local(): pl.pallas_call(functools.partial(kernel, n, keep), out_shape=(wide, wide,...]
where the time goes in v3:
time: 53.1 us; the launch traced here: 52.9 us
  Pallas kernels  51.6 us (97%)
  between operations  1.29 us (2%)
    pallas_call x1, Pallas kernels, local(): pl.pallas_call(functools.partial(kernel, n, keep), out_shape=(wide, wide,...  50.1 us
    pallas_call x1, Pallas kernels, local(): pl.pallas_call(finish, out_shape=(wide, wide, wide, thin), in_specs=[vmem...  1.54 us

profile of v3, /device:TPU:0, one launch (start us, length us, event | category | flops | bytes accessed | tf_op | source)
XLA Modules:
  0.0 52.9 jit_solution(16399042755242173141)
XLA Ops:
  1.3 50.1 %cg_step.1 = (f32[8,1024]{1,0:T(8,128)}, f32[8,1024]{1,0:T(8,128)}, f32[1,8]{1,0:T(1,128)}, f32[1,8]{1,0:T(1,128)}) custom-call(bf16[64,1024]{1,0:T(8,128)(2,1)} %points_ref.1, bf16[64,1024]{1,0:T(8,128)(2,1)} %landmarks_ref.1, f32[1024,1024]{1,0:T(8,128)} %chol_hbm.1, f32[1]{0:T(128)S(6)} %copy.12.ridge_ref, f32[8,1024]{1,0:T(8,128)} %residual_ref.3, ...), custom_call_target="tpu_custom_call" | custom-call | tf_op jit(solution)/shard_map/cg_step/pallas_call | solution.py:449
  51.4 1.5 %finish.1 = (f32[8,1024]{1,0:T(8,128)}, f32[8,1024]{1,0:T(8,128)}, f32[8,1024]{1,0:T(8,128)}, f32[1,8]{1,0:T(1,128)}) custom-call(f32[8,1024]{1,0:T(8,128)} %get-tuple-element.12.image_ref, f32[8,1024]{1,0:T(8,128)} %get-tuple-element.13.direction_ref, f32[1,8]{1,0:T(1,128)} %get-tuple-element.14.inner_ref, f32[1,8]{1,0:T(1,128)} %get-tuple-element.15.alpha_ref, ...), custom_call_target="tpu_custom_call" | custom-call | tf_op jit(solution)/shard_map/finish/pallas_call | solution.py:497

commit v4 on v3

--- a/solution.py
+++ b/solution.py
@@ -269,10 +269,7 @@
     shared = remote(shares, shares, share_sems.at[0], share_sems.at[1], partner)
     shared.start()
 
-    if keep:
-        make_block(me, me)
-
-    def relay(s, both):
+    def pass_on(s, both):
         near = row_of(pos - s, 0)
         remote(points_ref, points.at[near], point_fwd.at[near], point_recv.at[near], right).wait_recv()
         if both:
@@ -287,6 +284,7 @@
             def _():
                 remote(points.at[far], points.at[far], point_fwd.at[far], point_recv.at[far], left).start()
 
+    def build_lanes(s, both):
         def build(lane):
             def one(way, carry):
                 owner = row_of(pos - s + 2 * s * way, lane)
@@ -301,7 +299,8 @@
         build(0)
         build(1)
 
-    relay(1, True)
+    pass_on(1, True)
+    build_lanes(1, True)
     remote(points_ref, points.at[partner], point_side.at[partner], point_recv.at[partner], partner).wait_recv()
 
     other = inverse.at[pl.ds(share - first, share)]
@@ -319,6 +318,7 @@
         if b > 0:
             store_split(chol_parts, (slice(at, end), slice(0, at)), chol[at:end, :at])
 
+    pass_on(2, True)
     wait_all(lambda to: ag.at[me], ag, ag_sems)
     for piece in range(n):
         h, j = piece // tiles, piece % tiles
@@ -348,9 +348,10 @@
     inner_buf[me] = to_row(jnp.sum(precond * residual, axis=1, keepdims=True), TILE)
     send_all(lambda to: inner_buf.at[me], inner_buf, inner_sems)
 
+    pass_on(3, True)
     if keep:
         make_block(partner, partner)
-    lax.fori_loop(2, min(3, half), lambda s, carry: (relay(s, True), carry)[1], 0)
+    build_lanes(2, True)
     wait_all(lambda to: inner_buf.at[me], inner_buf, inner_sems)
     inner_row = jnp.sum(inner_buf[...], axis=0)
     inner_out[...] = inner_row[:, :outs]
@@ -360,8 +361,18 @@
     dirs[me] = direction_new.astype(jnp.bfloat16)
     send_all(lambda to: dirs.at[me], dirs, dir_sems)
 
-    lax.fori_loop(3, half, lambda s, carry: (relay(s, True), carry)[1], 0)
-    relay(half, False)
+    if keep:
+        make_block(me, me)
+    build_lanes(3, True)
+
+    def later(s, carry):
+        pass_on(s, True)
+        build_lanes(s, True)
+        return carry
+
+    lax.fori_loop(4, half, later, 0)
+    pass_on(half, False)
+    build_lanes(half, False)
 
     def image_part(owner, slot):
         if not keep:

time: 53.1 us -> 48.3 us (0.910)
  Pallas kernels: 51.6 us -> 46.8 us
    pallas_call x1, Pallas kernels: 50.1 us -> 45.3 us  [local(): pl.pallas_call(functools.partial(kernel, n, keep), out_shape=(wide, wide,...]
where the time goes in v4:
time: 48.3 us; the launch traced here: 48.1 us
  Pallas kernels  46.8 us (97%)
  between operations  1.29 us (3%)
    pallas_call x1, Pallas kernels, local(): pl.pallas_call(functools.partial(kernel, n, keep), out_shape=(wide, wide,...  45.3 us
    pallas_call x1, Pallas kernels, local(): pl.pallas_call(finish, out_shape=(wide, wide, wide, thin), in_specs=[vmem...  1.54 us

profile of v4, /device:TPU:0, one launch (start us, length us, event | category | flops | bytes accessed | tf_op | source)
XLA Modules:
  0.0 48.1 jit_solution(8279795752732260301)
XLA Ops:
  1.3 45.3 %cg_step.1 = (f32[8,1024]{1,0:T(8,128)}, f32[8,1024]{1,0:T(8,128)}, f32[1,8]{1,0:T(1,128)}, f32[1,8]{1,0:T(1,128)}) custom-call(bf16[64,1024]{1,0:T(8,128)(2,1)} %points_ref.1, bf16[64,1024]{1,0:T(8,128)(2,1)} %landmarks_ref.1, f32[1024,1024]{1,0:T(8,128)} %chol_hbm.1, f32[1]{0:T(128)S(6)} %copy.12.ridge_ref, f32[8,1024]{1,0:T(8,128)} %residual_ref.3, ...), custom_call_target="tpu_custom_call" | custom-call | tf_op jit(solution)/shard_map/cg_step/pallas_call | solution.py:460
  46.6 1.5 %finish.1 = (f32[8,1024]{1,0:T(8,128)}, f32[8,1024]{1,0:T(8,128)}, f32[8,1024]{1,0:T(8,128)}, f32[1,8]{1,0:T(1,128)}) custom-call(f32[8,1024]{1,0:T(8,128)} %get-tuple-element.12.image_ref, f32[8,1024]{1,0:T(8,128)} %get-tuple-element.13.direction_ref, f32[1,8]{1,0:T(1,128)} %get-tuple-element.14.inner_ref, f32[1,8]{1,0:T(1,128)} %get-tuple-element.15.alpha_ref, ...), custom_call_target="tpu_custom_call" | custom-call | tf_op jit(solution)/shard_map/finish/pallas_call | solution.py:508
